TPU v7x, 32 devices: a whole 2x2x4 slice. The times are simulated.
32 devices in a mesh: grp: 1, row: 32 (over z, y, x, core).
Axes of the slice: x: 2, y: 2, z: 4, core: 2. Of those that a mesh axis runs over, the one named last changes fastest.
Arguments:
- features: bfloat16 [64, 192, 2048], P(('grp', 'row')), may hold values from -6 to 6
- branch_kernel_weight: bfloat16 [2048, 10, 128], P('row'), may hold values from -0.046875 to 0.046875
- branch_norm_bias: float32 [2, 128], replicated, may hold values from -3 to 3
- merge_weight: bfloat16 [256, 256], P('row'), may hold values from -0.375 to 0.375
- merge_bias: float32 [256], replicated, may hold values from -3 to 3
- cotangent: bfloat16 [64, 192, 256], P(('grp', 'row')), may hold values from -24 to 24
Outputs:
- merged: bfloat16 [64, 192, 256], P(('grp', 'row'))
- input_grad: bfloat16 [64, 192, 2048], P(('grp', 'row'))
- branch_kernel_gradient: float32 [2048, 10, 128], P(('grp', 'row'))
- grad_merge: float32 [256, 256], P(('grp', 'row'))
All inputs are finite; a program needn't handle non-finite values.
Results may differ from a plain program's by a relative error of at most 0.023.
The roundings to bfloat16 on the way count: a program that leaves them out, or rounds other values in their place, can miss the bound.
Values may be sent and summed in bfloat16 or wider, within the bound.
No kernel may reach another device: no remote copies, remote signals or barrier semaphores. Data moves between devices by JAX's collectives and lax.ppermute only.
A program may use at most 128 MiB of HBM per device.

v0:
```python
import math
import jax
import jax.numpy as jnp
from jax import lax
from jax.sharding import PartitionSpec as P

DILATION_RATE = 18


def passed_along(block, axis, distance):
    devices = range(lax.axis_size(axis))
    route = [(i - distance, i) for i in devices if i - distance in devices]
    return lax.ppermute(block, axis, route)


def transposed_product(left, right):
    return lax.dot_general(
        left, right, (((0,), (0,)), ((), ())), preferred_element_type=jnp.float32
    )


def ndot(left, right):
    return lax.dot_general(
        left, right, (((1,), (1,)), ((), ())), preferred_element_type=jnp.float32
    )


def gather_feature_rows(row_block, device_step):
    return passed_along(row_block, "row", device_step)


def gather_gradient_rows(row_block, device_step):
    return passed_along(row_block, "row", device_step)


def load_row_block(row_block, row_offset, pull_rows):
    block_row_count = row_block.shape[0]
    device_off, inner_off = divmod(row_offset, block_row_count)
    return pull_rows(row_block, -device_off)


def on_device(
    features, branch_kernel_weight, branch_norm_bias, merge_weight, merge_bias, cotangent
):
    block_row_count = features.shape[0]
    width_columns = features.shape[1]
    channel_count = features.shape[2]
    branch_channel_width = branch_kernel_weight.shape[2]
    pixel_count = block_row_count * width_columns
    gradient_scale = 1.0 / math.sqrt(block_row_count * lax.axis_size("row") * width_columns)
    flattened = features.reshape(pixel_count, channel_count)
    row_groups = [
        load_row_block(features, -DILATION_RATE, gather_feature_rows),
        features,
        load_row_block(features, DILATION_RATE, gather_feature_rows),
    ]
    padded_row_groups = [
        jnp.pad(row_group, ((0, 0), (DILATION_RATE, DILATION_RATE), (0, 0)))
        for row_group in row_groups
    ]
    tap_windows = [
        padded_row_groups[tap_number // 3][
            :, tap_number % 3 * DILATION_RATE : tap_number % 3 * DILATION_RATE + width_columns
        ].reshape(pixel_count, channel_count)
        for tap_number in range(9)
    ]
    whole_branch, whole_merge = (
        lax.all_gather(branch_kernel_weight, "row", axis=0, tiled=True),
        lax.all_gather(merge_weight, "row", axis=0, tiled=True),
    )
    z_one = jnp.dot(flattened, whole_branch[:, 0, :], preferred_element_type=jnp.float32)
    dilated_preactivation = jnp.zeros((pixel_count, branch_channel_width), jnp.float32)
    for tap_number in range(9):
        dilated_preactivation = dilated_preactivation + jnp.dot(
            tap_windows[tap_number],
            whole_branch[:, 1 + tap_number, :],
            preferred_element_type=jnp.float32,
        )
    pointwise_activation = jnp.maximum(z_one + branch_norm_bias[0], 0.0).astype(jnp.bfloat16)
    dilated_activation = jnp.maximum(dilated_preactivation + branch_norm_bias[1], 0.0).astype(
        jnp.bfloat16
    )
    combined = jnp.concatenate([pointwise_activation, dilated_activation], axis=1)
    merged = jnp.maximum(
        jnp.dot(combined, whole_merge, preferred_element_type=jnp.float32) + merge_bias, 0.0
    ).astype(jnp.bfloat16)
    grad_out = jnp.where(
        merged > 0, cotangent.reshape(pixel_count, merged.shape[1]), jnp.zeros((), jnp.bfloat16)
    )
    grad_merge = (
        lax.psum_scatter(
            transposed_product(combined, grad_out), "row", scatter_dimension=0, tiled=True
        )
        * gradient_scale
    )
    backward_pass = ndot(grad_out, whole_merge)
    pointwise_gradient = jnp.where(
        pointwise_activation > 0, backward_pass[:, :branch_channel_width], 0.0
    ).astype(jnp.bfloat16)
    dilated_gradient = jnp.where(
        dilated_activation > 0, backward_pass[:, branch_channel_width:], 0.0
    ).astype(jnp.bfloat16)
    gradient_map = dilated_gradient.reshape(block_row_count, width_columns, branch_channel_width)
    gradient_row_groups = [
        load_row_block(gradient_map, DILATION_RATE, gather_gradient_rows),
        gradient_map,
        load_row_block(gradient_map, -DILATION_RATE, gather_gradient_rows),
    ]
    padded_gradient = [
        jnp.pad(gradient_row_group, ((0, 0), (DILATION_RATE, DILATION_RATE), (0, 0)))
        for gradient_row_group in gradient_row_groups
    ]
    grad_views = [
        padded_gradient[tap_number // 3][
            :,
            (2 - tap_number % 3) * DILATION_RATE : (2 - tap_number % 3) * DILATION_RATE
            + width_columns,
        ].reshape(pixel_count, branch_channel_width)
        for tap_number in range(9)
    ]
    pieces_list = [transposed_product(flattened, pointwise_gradient)]
    for branch_tap_number in range(9):
        pieces_list.append(transposed_product(tap_windows[branch_tap_number], dilated_gradient))
    branch_kernel_gradient = (
        lax.psum_scatter(jnp.stack(pieces_list, axis=1), "row", scatter_dimension=0, tiled=True)
        * gradient_scale
    )
    input_total = ndot(pointwise_gradient, whole_branch[:, 0, :])
    for tap_number in range(9):
        input_total = input_total + ndot(grad_views[tap_number], whole_branch[:, 1 + tap_number, :])
    input_grad = input_total.astype(jnp.bfloat16).reshape(
        block_row_count, width_columns, channel_count
    )
    return (
        merged.reshape(block_row_count, width_columns, merged.shape[1]),
        input_grad,
        branch_kernel_gradient,
        grad_merge,
    )


def solution(mesh):
    placed = (
        P(("grp", "row"), None, None),
        P("row", None, None),
        P(),
        P("row", None),
        P(),
        P(("grp", "row"), None, None),
    )
    return jax.shard_map(
        on_device,
        mesh=mesh,
        in_specs=placed,
        out_specs=(
            P(("grp", "row"), None, None),
            P(("grp", "row"), None, None),
            P(("grp", "row"), None, None),
            P(("grp", "row"), None),
        ),
        check_vma=False,
    )
```

profile of v0, /device:TPU:14, one launch (start us, length us, event | category | flops | bytes accessed | tf_op | source)
XLA Modules:
  0.0 479.6 jit_solution(15988764721342532943)
XLA Ops:
  7.9 2.9 collective-permute-start
  10.9 3.6 collective-permute-start.1
  14.5 101.5 %all_gather.7 = bf16[256,256]{1,0:T(8,128)(2,1)S(1)} all-gather(bf16[8,256]{1,0:T(8,128)(2,1)} %param.9), channel_id=1, replica_groups=mesh['grp'=1,'row'=32] {'row'}, dimensions={0}, use_global_device_ids=true | all-gather | bytes 135168 | tf_op jit(solution)/shard_map/all_gather | solution.py:69
  116.8 4.3 pad_slice_fusion.2
  121.2 2.3 pad_slice_fusion.5
  123.5 1.8 pad_slice_fusion.1
  125.3 2.7 fusion.26
  128.0 2.5 fusion.28
  130.6 1.7 fusion.24
  141.4 3.0 fusion.5
  147.2 1.5 fusion.3
  151.6 1.5 fusion.1
  156.3 17.6 %copy.65 = f32[2048,10,128]{2,1,0:T(8,128)} copy(f32[2048,10,128]{0,2,1:T(8,128)} %fusion) | data formatting | bytes 20971520 | tf_op jit(solution)/shard_map/stack | solution.py:125
  174.0 1.9 collective-permute-start.2
  175.9 3.6 collective-permute-start.3
  179.6 1.8 fusion.29
  181.4 1.7 fusion.27
  183.1 3.3 fusion.21
  188.3 2.3 fusion.31
  190.6 2.3 fusion.23
  192.8 2.3 fusion.32
  195.1 8.0 %add_convert_fusion = bf16[384,2048]{1,0:T(8,128)(2,1)} fusion(f32[384,2048]{1,0:T(8,128)} %fusion.32, f32[384,2048]{1,0:T(8,128)} %fusion.31, f32[384,2048]{1,0:T(8,128)S(1)} %fusion.30, f32[384,2048]{1,0:T(8,128)S(1)} %fusion.29, f32[384,2048]{1,0:T(8,128)S(1)} %fusion.27, f32[384,2048]{1,0:T(8,128)S(1)} %fusion.25, f32[384,2048]{1,0:T(8,128)} %fusion.23, ...), kind=kOutput, calls=%fused_computation | convolution fusion | flops 209190912 | bytes 30507008 | tf_op jit(solution)/shard_map/dot_general | solution.py:23
  203.1 52.5 %reduce-scatter.5.cloned.1.call-done = f32[8,256]{1,0:T(8,128)} async-done(((f32[256,256]{1,0:T(8,128)}), f32[8,256]{1,0:T(8,128)}) %reduce-scatter.5.cloned.1.call-update) | async-done | bytes 8208 | tf_op jit(solution)/shard_map/reduce_scatter | solution.py:91
  256.8 214.3 %reduce-scatter.3.cloned.1.call-done = f32[64,10,128]{2,1,0:T(8,128)} async-done(((f32[2048,10,128]{2,1,0:T(8,128)}), f32[64,10,128]{2,1,0:T(8,128)}) %reduce-scatter.3.cloned.1.call-update) | async-done | bytes 327696 | tf_op jit(solution)/shard_map/reduce_scatter | solution.py:125
  (79 shorter events, 24.5 us)
Async XLA Ops:
  7.2 118.1 %all-gather.2.cloned.1.call-start = ((), (), s32[]{:S(2)}) async-start(), calls=%async_computation.2 | async-start | bytes 5406720 | tf_op jit(solution)/shard_map/all_gather | solution.py:68
  7.9 247.6 %reduce-scatter.5.cloned.1.call-start = ((), (), s32[]{:S(2)}) async-start(), calls=%async_computation.4 | async-start | bytes 270336 | tf_op jit(solution)/shard_map/reduce_scatter | solution.py:91
  7.9 113.2 %collective-permute-start = (bf16[2,192,2048]{2,1,0:T(8,128)(2,1)}, bf16[2,192,2048]{2,1,0:T(8,128)(2,1)S(1)}, u32[]{:S(2)}, u32[]{:S(2)}) collective-permute-start(bf16[2,192,2048]{2,1,0:T(8,128)(2,1)} %param.6), channel_id=1, source_target_pairs={{0,9},{1,10},{2,11},{3,12},{4,13},{5,14},{6,15},{7,16},{8,17},{9,1... | collective-permute-start | bytes 4718600 | tf_op jit(solution)/shard_map/ppermute | solution.py:13
  10.9 112.6 %collective-permute-start.1 = (bf16[2,192,2048]{2,1,0:T(8,128)(2,1)}, bf16[2,192,2048]{2,1,0:T(8,128)(2,1)S(1)}, u32[]{:S(2)}, u32[]{:S(2)}) collective-permute-start(bf16[2,192,2048]{2,1,0:T(8,128)(2,1)} %param.6), channel_id=1, source_target_pairs={{9,0},{10,1},{11,2},{12,3},{13,4},{14,5},{15,6},{16,7},{17,8},{18,... | collective-permute-start | bytes 4718600 | tf_op jit(solution)/shard_map/ppermute | solution.py:13
  116.1 20.8 %copy-start.14 = (bf16[256,256]{1,0:T(8,128)(2,1)}, bf16[256,256]{1,0:T(8,128)(2,1)S(1)}, u32[]{:S(2)}) copy-start(bf16[256,256]{1,0:T(8,128)(2,1)S(1)} %all_gather.7) | copy-start | bytes 393220
  121.1 2.3 copy-start.4
  125.3 7.0 %copy-start.2 = (bf16[2,192,2048]{2,1,0:T(8,128)(2,1)}, bf16[2,192,2048]{2,1,0:T(8,128)(2,1)S(1)}, u32[]{:S(2)}) copy-start(bf16[2,192,2048]{2,1,0:T(8,128)(2,1)S(1)} %get-tuple-element.17) | copy-start | bytes 4718596
  125.3 5.3 %copy-start.5 = (bf16[2,192,2048]{2,1,0:T(8,128)(2,1)S(1)}, bf16[2,192,2048]{2,1,0:T(8,128)(2,1)}, u32[]{:S(2)}) copy-start(bf16[2,192,2048]{2,1,0:T(8,128)(2,1)} %copy-done.4) | copy-start | bytes 4718596
  125.3 7.0 %copy-start.1 = (bf16[2048,10,128]{2,0,1:T(8,128)(2,1)S(1)}, bf16[2048,10,128]{2,0,1:T(8,128)(2,1)}, u32[]{:S(2)}) copy-start(bf16[2048,10,128]{2,0,1:T(8,128)(2,1)} %all-gather.2.cloned.1.call-done) | copy-start | bytes 15728644
  130.6 3.0 copy-start.13
  133.0 1.4 copy-start
  133.6 2.0 copy-start.7
  134.4 1.9 copy-start.10
  141.4 3.0 copy-start.6
  141.4 4.4 copy-start.12
  144.3 2.9 copy-start.9
  147.2 2.9 copy-start.8
  148.7 2.9 copy-start.11
  151.6 3.3 copy-start.3
  153.1 318.0 %reduce-scatter.3.cloned.1.call-start = ((), (), s32[]{:S(2)}) async-start(), calls=%async_computation.3 | async-start | bytes 17301504 | tf_op jit(solution)/shard_map/reduce_scatter | solution.py:125
  174.0 13.0 %collective-permute-start.2 = (bf16[2,192,128]{2,1,0:T(8,128)(2,1)S(1)}, bf16[2,192,128]{2,1,0:T(8,128)(2,1)S(1)}, u32[]{:S(2)}, u32[]{:S(2)}) collective-permute-start(bf16[2,192,128]{2,1,0:T(8,128)(2,1)S(1)} %bitcast.182), channel_id=1, source_target_pairs={{9,0},{10,1},{11,2},{12,3},{13,4},{14,5},{15,6},{16,7},{17,8},{18,... | collective-permute-start | bytes 294920 | tf_op jit(solution)/shard_map/ppermute | solution.py:13
  175.9 11.1 %collective-permute-start.3 = (bf16[2,192,128]{2,1,0:T(8,128)(2,1)S(1)}, bf16[2,192,128]{2,1,0:T(8,128)(2,1)S(1)}, u32[]{:S(2)}, u32[]{:S(2)}) collective-permute-start(bf16[2,192,128]{2,1,0:T(8,128)(2,1)S(1)} %bitcast.183), channel_id=1, source_target_pairs={{0,9},{1,10},{2,11},{3,12},{4,13},{5,14},{6,15},{7,16},{8,17},{9,1... | collective-permute-start | bytes 294920 | tf_op jit(solution)/shard_map/ppermute | solution.py:13
  179.6 6.8 %slice-start = ((s8[5242880]{0:T(1024)(128)(4,1)}), s8[4194304]{0:T(1024)(128)(4,1)S(1)}, s32[]{:S(2)}) async-start(s8[5242880]{0:T(1024)(128)(4,1)} %bitcast.162), calls=%async_computation.5 | async-start | bytes 8388608
  181.4 5.0 %slice-start.1 = ((s8[5242880]{0:T(1024)(128)(4,1)}), s8[1048576]{0:T(1024)(128)(4,1)S(1)}, s32[]{:S(2)}) async-start(s8[5242880]{0:T(1024)(128)(4,1)} %bitcast.162), calls=%async_computation.6 | async-start | bytes 2097152
  (2 other events, 2.5 us)
Sparse Core Ops, SparseCore 0:
  10.9 78.9 all-gather.1
  153.3 102.2 reduce-scatter.4
  257.9 213.1 reduce-scatter.2
where the time goes:
time: 480 us
  waiting for transfers between devices  268 us (56%)
  blocking collectives  102 us (21%)
  matrix products  53.5 us (11%)
  local copies, waits for them, and re-layouts  28.1 us (6%)
  between operations  14.1 us (3%)
  starting transfers between devices  12.4 us (3%)
    reduce_scatter x1, waiting for transfers between devices, on_device(): lax.psum_scatter(jnp.stack(pieces_list, axis=1), 'row', scatter_dimension...  214 us
    all_gather x1, blocking collectives, on_device(): lax.all_gather(merge_weight, 'row', axis=0, tiled=True)  102 us
    reduce_scatter x1, waiting for transfers between devices, on_device(): lax.psum_scatter(transposed_product(combined, grad_out), 'row', scatter_d...  52.5 us
    dot_general x11, matrix products, ndot(): lax.dot_general(left, right, (((1,), (1,)), ((), ())), preferred_element_...  24.4 us
    another operation x1, local copies, waits for them, and re-layouts, on_device(): jnp.stack(pieces_list, axis=1)  17.6 us
    dot_general x11, matrix products, transposed_product(): lax.dot_general(left, right, (((0,), (0,)), ((), ())), preferred_element_...  16.9 us
    ppermute x4, starting transfers between devices, passed_along(): return lax.ppermute(block, axis, route)  12.1 us
    dot_general x9, matrix products, on_device(): jnp.dot(tap_windows[tap_number], whole_branch[:, 1 + tap_number, :], pref...  10.6 us
  transfers between devices with their start and end apart: 7, of which 2 were waited for; matrix products, arithmetic and copies ran while one was open for 11% of the time, Pallas kernels for 0%

commit v1 on v0

--- a/solution.py
+++ b/solution.py
@@ -5,6 +5,18 @@
 from jax.sharding import PartitionSpec as P
 
 DILATION_RATE = 18
+
+
+def gather_by_bits(x, axis, dim):
+    ways, here = (lax.axis_size(axis), lax.axis_index(axis))
+    grown, reach = (x, 1)
+    while reach < ways:
+        theirs = lax.ppermute(grown, axis, [(d, d ^ reach) for d in range(ways)])
+        mine_first = jnp.concatenate([grown, theirs], axis=dim)
+        theirs_first = jnp.concatenate([theirs, grown], axis=dim)
+        grown = jnp.where(here & reach == 0, mine_first, theirs_first)
+        reach = 2 * reach
+    return grown
 
 
 def passed_along(block, axis, distance):
@@ -66,7 +78,7 @@
     ]
     whole_branch, whole_merge = (
         lax.all_gather(branch_kernel_weight, "row", axis=0, tiled=True),
-        lax.all_gather(merge_weight, "row", axis=0, tiled=True),
+        gather_by_bits(merge_weight, "row", 0),
     )
     z_one = jnp.dot(flattened, whole_branch[:, 0, :], preferred_element_type=jnp.float32)
     dilated_preactivation = jnp.zeros((pixel_count, branch_channel_width), jnp.float32)

time: 480 us -> 451 us (0.940)
  blocking collectives: 102 us -> 0 us
  waiting for transfers between devices: 268 us -> 336 us
    all_gather x1 -> x0, blocking collectives: 102 us -> none  [on_device(): lax.all_gather(merge_weight, 'row', axis=0, tiled=True)]
    ppermute x0 -> x5, waiting for transfers between devices: none -> 38 us  [gather_by_bits(): theirs = lax.ppermute(grown, axis, [(d, d ^ reach) for d in range(ways)])]
    ppermute x4, waiting for transfers between devices: 0.01 us -> 27.9 us  [passed_along(): return lax.ppermute(block, axis, route)]
  transfers between devices with their start and end apart: 7 -> 12, of which waited for: 2 -> 6; matrix products, arithmetic and copies ran while one was open for 11% -> 15% of each run, Pallas kernels for 0% -> 0%
where the time goes in v1:
time: 451 us; the launch traced here: 450 us
  waiting for transfers between devices  336 us (75%)
  matrix products  52.9 us (12%)
  local copies, waits for them, and re-layouts  28 us (6%)
  starting transfers between devices  15.6 us (3%)
  between operations  14.1 us (3%)
    reduce_scatter x1, waiting for transfers between devices, on_device(): lax.psum_scatter(jnp.stack(pieces_list, axis=1), 'row', scatter_dimension...  214 us
    reduce_scatter x1, waiting for transfers between devices, on_device(): lax.psum_scatter(transposed_product(combined, grad_out), 'row', scatter_d...  55.2 us
    ppermute x5, waiting for transfers between devices, gather_by_bits(): theirs = lax.ppermute(grown, axis, [(d, d ^ reach) for d in range(ways)])  38 us
    ppermute x4, waiting for transfers between devices, passed_along(): return lax.ppermute(block, axis, route)  27.9 us
    dot_general x11, matrix products, ndot(): lax.dot_general(left, right, (((1,), (1,)), ((), ())), preferred_element_...  24.4 us
    another operation x1, local copies, waits for them, and re-layouts, on_device(): jnp.stack(pieces_list, axis=1)  17.6 us
    dot_general x11, matrix products, transposed_product(): lax.dot_general(left, right, (((0,), (0,)), ((), ())), preferred_element_...  16.9 us
    ppermute x4, starting transfers between devices, passed_along(): return lax.ppermute(block, axis, route)  12.1 us
  transfers between devices with their start and end apart: 12, of which 6 were waited for; matrix products, arithmetic and copies ran while one was open for 15% of the time, Pallas kernels for 0%

profile of v1, /device:TPU:14, one launch (start us, length us, event | category | flops | bytes accessed | tf_op | source)
XLA Modules:
  0.0 449.9 jit_solution(12066763118177373410)
XLA Ops:
  8.0 2.9 collective-permute-start
  10.9 3.6 collective-permute-start.1
  18.2 5.6 %collective-permute-done.3 = bf16[16,256]{1,0:T(8,128)(2,1)S(1)} collective-permute-done((bf16[16,256]{1,0:T(8,128)(2,1)S(1)}, bf16[16,256]{1,0:T(8,128)(2,1)S(1)}, u32[]{:S(2)}, u32[]{:S(2)}) %collective-permute-start.3) | collective-permute-done | bytes 8224 | tf_op jit(solution)/shard_map/ppermute | solution.py:14
  23.8 4.3 pad_slice_fusion.2
  28.2 31.1 %collective-permute-done.5 = bf16[64,256]{1,0:T(8,128)(2,1)S(1)} collective-permute-done((bf16[64,256]{1,0:T(8,128)(2,1)S(1)}, bf16[64,256]{1,0:T(8,128)(2,1)S(1)}, u32[]{:S(2)}, u32[]{:S(2)}) %collective-permute-start.5) | collective-permute-done | bytes 32800 | tf_op jit(solution)/shard_map/ppermute | solution.py:14
  60.9 27.8 %collective-permute-done = bf16[2,192,2048]{2,1,0:T(8,128)(2,1)S(1)} collective-permute-done((bf16[2,192,2048]{2,1,0:T(8,128)(2,1)}, bf16[2,192,2048]{2,1,0:T(8,128)(2,1)S(1)}, u32[]{:S(2)}, u32[]{:S(2)}) %collective-permute-start) | collective-permute-done | bytes 1572896 | tf_op jit(solution)/shard_map/ppermute | solution.py:25
  88.8 2.3 pad_slice_fusion.5
  91.1 2.3 pad_slice_fusion.1
  93.4 2.2 fusion.26
  95.6 2.5 fusion.28
  98.1 1.7 fusion.24
  109.1 3.0 fusion.5
  123.9 17.6 %copy.65 = f32[2048,10,128]{2,1,0:T(8,128)} copy(f32[2048,10,128]{0,2,1:T(8,128)} %fusion) | data formatting | bytes 20971520 | tf_op jit(solution)/shard_map/stack | solution.py:137
  141.7 1.9 collective-permute-start.7
  143.6 3.6 collective-permute-start.8
  147.3 1.8 fusion.29
  149.1 1.7 fusion.27
  150.8 3.3 fusion.21
  156.0 2.3 fusion.31
  158.2 2.3 fusion.23
  160.5 2.3 fusion.32
  162.8 8.0 %add_convert_fusion = bf16[384,2048]{1,0:T(8,128)(2,1)} fusion(f32[384,2048]{1,0:T(8,128)} %fusion.32, f32[384,2048]{1,0:T(8,128)} %fusion.31, f32[384,2048]{1,0:T(8,128)S(1)} %fusion.30, f32[384,2048]{1,0:T(8,128)S(1)} %fusion.29, f32[384,2048]{1,0:T(8,128)S(1)} %fusion.27, f32[384,2048]{1,0:T(8,128)S(1)} %fusion.25, f32[384,2048]{1,0:T(8,128)} %fusion.23, ...), kind=kOutput, calls=%fused_computation | convolution fusion | flops 209190912 | bytes 30507008 | tf_op jit(solution)/shard_map/dot_general | solution.py:35
  170.7 55.2 %reduce-scatter.5.cloned.1.call-done = f32[8,256]{1,0:T(8,128)} async-done(((f32[256,256]{1,0:T(8,128)}), f32[8,256]{1,0:T(8,128)}) %reduce-scatter.5.cloned.1.call-update) | async-done | bytes 8208 | tf_op jit(solution)/shard_map/reduce_scatter | solution.py:103
  227.2 214.2 %reduce-scatter.3.cloned.1.call-done = f32[64,10,128]{2,1,0:T(8,128)} async-done(((f32[2048,10,128]{2,1,0:T(8,128)}), f32[64,10,128]{2,1,0:T(8,128)}) %reduce-scatter.3.cloned.1.call-update) | async-done | bytes 327696 | tf_op jit(solution)/shard_map/reduce_scatter | solution.py:137
  (92 shorter events, 32.3 us)
Async XLA Ops:
  7.2 21.0 %copy-start.13 = (f32[2,128]{1,0:T(2,128)S(1)}, f32[2,128]{1,0:T(2,128)}, u32[]{:S(2)}) copy-start(f32[2,128]{1,0:T(2,128)} %param.8) | copy-start | bytes 3076
  7.2 86.2 %all-gather.2.cloned.1.call-start = ((), (), s32[]{:S(2)}) async-start(), calls=%async_computation.2 | async-start | bytes 5406720 | tf_op jit(solution)/shard_map/all_gather | solution.py:80
  7.9 218.0 %reduce-scatter.5.cloned.1.call-start = ((), (), s32[]{:S(2)}) async-start(), calls=%async_computation.4 | async-start | bytes 270336 | tf_op jit(solution)/shard_map/reduce_scatter | solution.py:103
  8.0 80.8 %collective-permute-start = (bf16[2,192,2048]{2,1,0:T(8,128)(2,1)}, bf16[2,192,2048]{2,1,0:T(8,128)(2,1)S(1)}, u32[]{:S(2)}, u32[]{:S(2)}) collective-permute-start(bf16[2,192,2048]{2,1,0:T(8,128)(2,1)} %param.6), channel_id=1, source_target_pairs={{0,9},{1,10},{2,11},{3,12},{4,13},{5,14},{6,15},{7,16},{8,17},{9,1... | collective-permute-start | bytes 4718600 | tf_op jit(solution)/shard_map/ppermute | solution.py:25
  10.9 80.2 %collective-permute-start.1 = (bf16[2,192,2048]{2,1,0:T(8,128)(2,1)}, bf16[2,192,2048]{2,1,0:T(8,128)(2,1)S(1)}, u32[]{:S(2)}, u32[]{:S(2)}) collective-permute-start(bf16[2,192,2048]{2,1,0:T(8,128)(2,1)} %param.6), channel_id=1, source_target_pairs={{9,0},{10,1},{11,2},{12,3},{13,4},{14,5},{15,6},{16,7},{17,8},{18,... | collective-permute-start | bytes 4718600 | tf_op jit(solution)/shard_map/ppermute | solution.py:25
  14.5 1.4 collective-permute-start.2
  16.7 7.0 %collective-permute-start.3 = (bf16[16,256]{1,0:T(8,128)(2,1)S(1)}, bf16[16,256]{1,0:T(8,128)(2,1)S(1)}, u32[]{:S(2)}, u32[]{:S(2)}) collective-permute-start(bf16[16,256]{1,0:T(8,128)(2,1)S(1)} %maximum_select_fusion.6), channel_id=1, source_target_pairs={{0,2},{1,3},{2,0},{3,1},{4,6},{5,7},{6,4},{7,5},{8,10},{9,11},{10,... | collective-permute-start | bytes 24584 | tf_op jit(solution)/shard_map/ppermute | solution.py:14
  23.8 4.3 collective-permute-start.4
  28.1 31.2 %collective-permute-start.5 = (bf16[64,256]{1,0:T(8,128)(2,1)S(1)}, bf16[64,256]{1,0:T(8,128)(2,1)S(1)}, u32[]{:S(2)}, u32[]{:S(2)}) collective-permute-start(bf16[64,256]{1,0:T(8,128)(2,1)S(1)} %maximum_select_fusion.2), channel_id=1, source_target_pairs={{0,8},{1,9},{2,10},{3,11},{4,12},{5,13},{6,14},{7,15},{8,0},{9,1},... | collective-permute-start | bytes 98312 | tf_op jit(solution)/shard_map/ppermute | solution.py:14
  59.3 45.2 %collective-permute-start.6 = (bf16[128,256]{1,0:T(8,128)(2,1)S(1)}, bf16[128,256]{1,0:T(8,128)(2,1)S(1)}, u32[]{:S(2)}, u32[]{:S(2)}) collective-permute-start(bf16[128,256]{1,0:T(8,128)(2,1)S(1)} %maximum_select_fusion.1), channel_id=1, source_target_pairs={{0,16},{1,17},{2,18},{3,19},{4,20},{5,21},{6,22},{7,23},{8,24},{9,... | collective-permute-start | bytes 196616 | tf_op jit(solution)/shard_map/ppermute | solution.py:14
  88.8 9.4 %copy-start.2 = (bf16[2,192,2048]{2,1,0:T(8,128)(2,1)}, bf16[2,192,2048]{2,1,0:T(8,128)(2,1)S(1)}, u32[]{:S(2)}) copy-start(bf16[2,192,2048]{2,1,0:T(8,128)(2,1)S(1)} %collective-permute-done) | copy-start | bytes 4718596
  93.4 6.5 %copy-start.1 = (bf16[2048,10,128]{2,0,1:T(8,128)(2,1)S(1)}, bf16[2048,10,128]{2,0,1:T(8,128)(2,1)}, u32[]{:S(2)}) copy-start(bf16[2048,10,128]{2,0,1:T(8,128)(2,1)} %all-gather.2.cloned.1.call-done) | copy-start | bytes 15728644
  93.4 6.5 %copy-start.7 = (bf16[2,192,2048]{2,1,0:T(8,128)(2,1)S(1)}, bf16[2,192,2048]{2,1,0:T(8,128)(2,1)}, u32[]{:S(2)}) copy-start(bf16[2,192,2048]{2,1,0:T(8,128)(2,1)} %get-tuple-element.17) | copy-start | bytes 4718596
  98.1 3.0 copy-start.12
  109.1 3.0 copy-start.3
  109.1 4.4 copy-start.11
  112.0 2.9 copy-start.6
  114.9 2.9 copy-start.5
  119.3 3.2 copy-start.8
  120.9 320.6 %reduce-scatter.3.cloned.1.call-start = ((), (), s32[]{:S(2)}) async-start(), calls=%async_computation.3 | async-start | bytes 17301504 | tf_op jit(solution)/shard_map/reduce_scatter | solution.py:137
  141.7 13.0 %collective-permute-start.7 = (bf16[2,192,128]{2,1,0:T(8,128)(2,1)S(1)}, bf16[2,192,128]{2,1,0:T(8,128)(2,1)S(1)}, u32[]{:S(2)}, u32[]{:S(2)}) collective-permute-start(bf16[2,192,128]{2,1,0:T(8,128)(2,1)S(1)} %bitcast.180), channel_id=1, source_target_pairs={{9,0},{10,1},{11,2},{12,3},{13,4},{14,5},{15,6},{16,7},{17,8},{18,... | collective-permute-start | bytes 294920 | tf_op jit(solution)/shard_map/ppermute | solution.py:25
  143.6 11.2 %collective-permute-start.8 = (bf16[2,192,128]{2,1,0:T(8,128)(2,1)S(1)}, bf16[2,192,128]{2,1,0:T(8,128)(2,1)S(1)}, u32[]{:S(2)}, u32[]{:S(2)}) collective-permute-start(bf16[2,192,128]{2,1,0:T(8,128)(2,1)S(1)} %bitcast.181), channel_id=1, source_target_pairs={{0,9},{1,10},{2,11},{3,12},{4,13},{5,14},{6,15},{7,16},{8,17},{9,1... | collective-permute-start | bytes 294920 | tf_op jit(solution)/shard_map/ppermute | solution.py:25
  147.3 6.8 %slice-start = ((s8[5242880]{0:T(1024)(128)(4,1)}), s8[4194304]{0:T(1024)(128)(4,1)S(1)}, s32[]{:S(2)}) async-start(s8[5242880]{0:T(1024)(128)(4,1)} %bitcast.160), calls=%async_computation.5 | async-start | bytes 8388608
  149.1 5.0 %slice-start.1 = ((s8[5242880]{0:T(1024)(128)(4,1)}), s8[1048576]{0:T(1024)(128)(4,1)S(1)}, s32[]{:S(2)}) async-start(s8[5242880]{0:T(1024)(128)(4,1)} %bitcast.160), calls=%async_computation.6 | async-start | bytes 2097152
  (7 other events, 12.2 us)
Sparse Core Ops, SparseCore 0:
  10.9 79.3 all-gather.1
  121.0 104.8 reduce-scatter.4
  228.3 213.0 reduce-scatter.2
